TPU v7x, 32 devices: a whole 2x2x4 slice. The times are simulated.
32 devices in a mesh: groups: 2 (over y), ctx: 4 (over z), head: 4 (over x, core).
Axes of the slice: x: 2, y: 2, z: 4, core: 2. Of those that a mesh axis runs over, the one named last changes fastest.
Arguments:
- query_rows: bfloat16 [3072, 3072], P(('groups', 'ctx', 'head')), parts along dimension 0, may hold values from -150 to 150
- key_rows: bfloat16 [3072, 3072], P(('groups', 'ctx', 'head')), parts along dimension 0, may hold values from -6 to 6
- value_rows: bfloat16 [3072, 3072], P(('groups', 'ctx', 'head')), parts along dimension 0, may hold values from -6 to 6
- tile_mask: int32 [8, 27], P(('groups', 'ctx')), parts along dimension 0, may hold values from 0 to 1, as said below
Outputs:
- attended: bfloat16 [3072, 3072], P(('groups', 'ctx', 'head')), parts along dimension 0
There are 2 independent parts, one for each index of `groups`. A program takes and returns all parts, laid end to end along the dimension named above; each array names one. Nothing has to cross between parts.
Inputs may be any that keep to these rules, and one draw needn't show every extreme that they name: `tile_mask`: entry o of row i is 1 only where the key tile of offset o lies inside the grid; entry 13 is always 1; a row has at most 4 ones, and some row has exactly 4.
All inputs are finite; a program needn't handle non-finite values.
Results may differ from a plain program's by a relative error of at most 0.0023.
Values may be sent and summed in bfloat16 or wider, within the bound.
No kernel may reach another device: no remote copies, remote signals or barrier semaphores. Data moves between devices by JAX's collectives and lax.ppermute only.
A program may use at most 64 MiB of HBM per device.

v0:
```python
import math
import jax
import jax.numpy as jnp
from jax import lax
from jax.sharding import PartitionSpec as P

HDIM = 128


def passed_along(block, axis, distance):
    devices = range(lax.axis_size(axis))
    route = [((i - distance) % len(devices), i) for i in devices]
    return lax.ppermute(block, axis, route)


def on_device(query_rows, key_rows, value_rows, tile_mask):
    cycle_size = lax.axis_size("ctx")
    grid_rows = max(2, cycle_size // 8)
    grid_cols = cycle_size // grid_rows
    query_local, key_local, value_local = (
        lax.all_to_all(query_rows, "head", split_axis=1, concat_axis=0, tiled=True),
        lax.all_to_all(key_rows, "head", split_axis=1, concat_axis=0, tiled=True),
        lax.all_to_all(value_rows, "head", split_axis=1, concat_axis=0, tiled=True),
    )
    feature_width = query_local.shape[1]
    head_count = feature_width // HDIM
    frames = tile_mask.shape[0]
    tile_len = query_local.shape[0] // frames
    key_value = jnp.stack([key_local, value_local]).reshape(2, frames, tile_len, feature_width)
    row_parts = [passed_along(key_value, "ctx", shift_by) for shift_by in (1, -1)]
    row_strip = jnp.stack([row_parts[0], key_value, row_parts[1]])
    column_parts = [
        passed_along(row_strip, "ctx", shift_by) for shift_by in (grid_cols, -grid_cols)
    ]
    window = jnp.stack([column_parts[0], row_strip, column_parts[1]])
    key_tiles = window[:, :, 0].reshape(9 * frames, tile_len, feature_width)
    value_tiles = window[:, :, 1].reshape(9 * frames, tile_len, feature_width)
    kept_mask = tile_mask == 1
    first_offset = 9
    slot_count = 9
    slot_order = jnp.arange(first_offset, first_offset + slot_count, dtype=jnp.int32)[None, :]
    slot_kept = kept_mask[:, first_offset : first_offset + slot_count]
    frame_ids = jnp.arange(frames, dtype=jnp.int32)[:, None]
    source_frame = jnp.clip(frame_ids + slot_order // 9 - 1, 0, frames - 1)
    source = slot_order % 9 * frames + source_frame
    kept_cols = jnp.repeat(slot_kept, tile_len, axis=1)[:, None, :]
    score_scale = 1.0 / math.sqrt(HDIM)

    def one_head(head_index):
        column_start = head_index * HDIM
        key_head = lax.dynamic_slice_in_dim(key_tiles, column_start, HDIM, 2)
        value_head = lax.dynamic_slice_in_dim(value_tiles, column_start, HDIM, 2)
        query_head = lax.dynamic_slice_in_dim(query_local, column_start, HDIM, 1).reshape(
            frames, tile_len, HDIM
        )
        picked_keys = jnp.take(key_head, source, axis=0).reshape(
            frames, slot_count * tile_len, HDIM
        )
        picked_values = jnp.take(value_head, source, axis=0).reshape(
            frames, slot_count * tile_len, HDIM
        )
        scores = (
            jnp.einsum("fqd,fkd->fqk", query_head, picked_keys, preferred_element_type=jnp.float32)
            * score_scale
        )
        row_peak = jnp.max(jnp.where(kept_cols, scores, -jnp.inf), axis=2, keepdims=True)
        weight = jnp.exp(jnp.where(kept_cols, scores - row_peak, -jnp.inf))
        row_total = jnp.sum(weight, axis=2, keepdims=True)
        rounded = weight.astype(jnp.bfloat16)
        mixed = jnp.einsum(
            "fqk,fkd->fqd", rounded, picked_values, preferred_element_type=jnp.float32
        )
        return (mixed / row_total).astype(jnp.bfloat16)

    result = lax.map(one_head, jnp.arange(head_count, dtype=jnp.int32))
    result = jnp.transpose(result, (1, 2, 0, 3)).reshape(frames * tile_len, feature_width)
    return lax.all_to_all(result, "head", split_axis=0, concat_axis=1, tiled=True)


def solution(mesh):
    placed = (
        P(("groups", "ctx", "head"), None),
        P(("groups", "ctx", "head"), None),
        P(("groups", "ctx", "head"), None),
        P(("groups", "ctx"), None),
    )
    return jax.shard_map(
        on_device,
        mesh=mesh,
        in_specs=placed,
        out_specs=P(("groups", "ctx", "head"), None),
        check_vma=False,
    )
```

profile of v0, /device:TPU:0, one launch (start us, length us, event | category | flops | bytes accessed | tf_op | source)
XLA Modules:
  0.0 327.5 jit_solution(2252575000279086143)
XLA Ops:
  0.0 1.9 copy.44
  1.9 4.2 %all-to-all-start.1 = ((bf16[96,4,768]{2,0,1:T(8,128)(2,1)}), bf16[96,4,768]{2,0,1:T(8,128)(2,1)S(1)}, u32[]{:S(2)}, u32[]{:S(2)}) async-start(bf16[96,4,768]{2,0,1:T(8,128)(2,1)} %bitcast.57), calls=%async_computation.1 | async-start | bytes 1179648 | tf_op jit(solution)/shard_map/all_to_all | solution.py:22
  6.2 1.1 copy.43
  7.3 8.4 %all-to-all-done.1 = bf16[96,4,768]{2,0,1:T(8,128)(2,1)S(1)} async-done(((bf16[96,4,768]{2,0,1:T(8,128)(2,1)}), bf16[96,4,768]{2,0,1:T(8,128)(2,1)S(1)}, u32[]{:S(2)}, u32[]{:S(2)}) %all-to-all-start.1) | async-done | bytes 589856 | tf_op jit(solution)/shard_map/all_to_all | solution.py:22
  15.7 11.9 %all_to_all.70 = bf16[96,4,768]{2,0,1:T(8,128)(2,1)S(1)} all-to-all(bf16[96,4,768]{2,0,1:T(8,128)(2,1)S(1)} %bitcast.84), channel_id=1, replica_groups=mesh['groups'=2,'ctx'=4,'head'=4] {'head'}, dimensions={1} | all-to-all | bytes 1179648 | tf_op jit(solution)/shard_map/all_to_all | solution.py:23
  27.7 2.3 collective-permute-start
  30.0 2.1 collective-permute-start.1
  32.1 26.8 %collective-permute-done = bf16[2,1,384,768]{3,2,0,1:T(8,128)(2,1)S(1)} collective-permute-done((bf16[2,1,384,768]{3,2,0,1:T(8,128)(2,1)S(1)}, bf16[2,1,384,768]{3,2,0,1:T(8,128)(2,1)S(1)}, u32[]{:S(2)}, u32[]{:S(2)}) %collective-permute-start) | collective-permute-done | bytes 1179680 | tf_op jit(solution)/shard_map/ppermute | solution.py:13
  58.9 23.7 %collective-permute-done.1 = bf16[2,1,384,768]{3,2,0,1:T(8,128)(2,1)S(1)} collective-permute-done((bf16[2,1,384,768]{3,2,0,1:T(8,128)(2,1)S(1)}, bf16[2,1,384,768]{3,2,0,1:T(8,128)(2,1)S(1)}, u32[]{:S(2)}, u32[]{:S(2)}) %collective-permute-start.1) | collective-permute-done | bytes 1179680 | tf_op jit(solution)/shard_map/ppermute | solution.py:13
  82.7 2.0 fusion.32
  84.7 1.3 collective-permute-start.2
  86.0 0.9 copy.45
  86.9 4.2 %all-to-all-start = ((bf16[96,4,768]{2,0,1:T(8,128)(2,1)}), bf16[96,4,768]{2,0,1:T(8,128)(2,1)}, u32[]{:S(2)}, u32[]{:S(2)}) async-start(bf16[96,4,768]{2,0,1:T(8,128)(2,1)} %bitcast.83), calls=%async_computation | async-start | bytes 1179648 | tf_op jit(solution)/shard_map/all_to_all | solution.py:21
  91.2 148.5 %collective-permute-done.2 = bf16[3,2,1,384,768]{4,3,1,0,2:T(8,128)(2,1)} collective-permute-done((bf16[3,2,1,384,768]{4,3,1,0,2:T(8,128)(2,1)}, bf16[3,2,1,384,768]{4,3,1,0,2:T(8,128)(2,1)}, u32[]{:S(2)}, u32[]{:S(2)}) %collective-permute-start.2) | collective-permute-done | bytes 3538976 | tf_op jit(solution)/shard_map/ppermute | solution.py:13
  239.6 8.4 %pad_maximum_fusion = bf16[3,3,2,1,384,768]{5,4,2,1,3,0:T(8,128)(2,1)} fusion(bf16[1,3,2,1,384,768]{5,4,2,1,3,0:T(8,128)(2,1)} %bitcast.11, bf16[1,3,2,1,384,768]{5,4,2,1,3,0:T(8,128)(2,1)S(1)} %get-tuple-element.112), kind=kLoop, calls=%fused_computation.36 | loop fusion | flops 10616832 | bytes 17694720 | tf_op jit(solution)/shard_map/stack | solution.py:35
  248.0 8.9 %fusion.36 = (bf16[3,3,1,1,384,768]{5,4,2,1,3,0:T(8,128)(2,1)}, bf16[3,3,1,1,384,768]{5,4,2,1,3,0:T(8,128)(2,1)}) fusion(bf16[3,3,2,1,384,768]{5,4,2,1,3,0:T(8,128)(2,1)} %pad_maximum_fusion), kind=kLoop, calls=%fused_computation.48 | loop fusion | bytes 21233664 | tf_op jit(solution)/shard_map/slice | solution.py:37
  256.9 55.6 %while.12 = (s32[]{:T(128)}, bf16[6,1,384,128]{3,2,1,0:T(8,128)(2,1)}, s32[6]{0:T(128)S(1)}, bf16[384,768]{1,0:T(8,128)(2,1)}, bf16[9,384,768]{2,1,0:T(8,128)(2,...) while((s32[]{:T(128)}, ...), condition=%wide.region_3.5_spmd.clone.clone, body=%wide.region_0.4_spmd.clone.clone.sunk | while | flops 692404736 | bytes 28541528 | solution.py:75
  258.2 1.6 constant_dynamic-slice_fusion.3
  259.8 0.7 gather_fusion
  261.6 1.9 select_reduce_fusion.2
  263.5 1.1 fusion.49
  264.6 1.6 fusion.50
  267.5 1.6 constant_dynamic-slice_fusion.3
  269.1 0.7 gather_fusion
  269.8 0.7 gather_fusion.1
  270.9 1.9 select_reduce_fusion.2
  272.7 1.1 fusion.49
  273.8 1.6 fusion.50
  276.7 1.6 constant_dynamic-slice_fusion.3
  278.3 0.7 gather_fusion
  280.1 1.9 select_reduce_fusion.2
  282.0 1.1 fusion.49
  283.1 1.6 fusion.50
  286.0 1.6 constant_dynamic-slice_fusion.3
  289.4 1.9 select_reduce_fusion.2
  291.3 1.1 fusion.49
  292.4 1.6 fusion.50
  295.3 1.6 constant_dynamic-slice_fusion.3
  298.7 1.9 select_reduce_fusion.2
  300.5 1.1 fusion.49
  301.6 1.6 fusion.50
  304.5 1.6 constant_dynamic-slice_fusion.3
  307.9 1.9 select_reduce_fusion.2
  309.8 1.1 fusion.49
  310.9 1.6 fusion.50
  312.5 1.5 copy.34
  314.7 11.9 %all_to_all.71 = bf16[4,96,768]{2,1,0:T(8,128)(2,1)S(1)} all-to-all(bf16[4,96,768]{2,1,0:T(8,128)(2,1)S(1)} %all_to_all.62), channel_id=1, replica_groups=mesh['groups'=2,'ctx'=4,'head'=4] {'head'}, dimensions={0} | all-to-all | bytes 1179648 | tf_op jit(solution)/shard_map/all_to_all | solution.py:77
  326.6 0.9 copy.39
  (61 shorter events, 12.6 us)
Async XLA Ops:
  1.9 13.8 %all-to-all-start.1 = ((bf16[96,4,768]{2,0,1:T(8,128)(2,1)}), bf16[96,4,768]{2,0,1:T(8,128)(2,1)S(1)}, u32[]{:S(2)}, u32[]{:S(2)}) async-start(bf16[96,4,768]{2,0,1:T(8,128)(2,1)} %bitcast.57), calls=%async_computation.1 | async-start | bytes 1179648 | tf_op jit(solution)/shard_map/all_to_all | solution.py:22
  27.7 31.2 %collective-permute-start = (bf16[2,1,384,768]{3,2,0,1:T(8,128)(2,1)S(1)}, bf16[2,1,384,768]{3,2,0,1:T(8,128)(2,1)S(1)}, u32[]{:S(2)}, u32[]{:S(2)}) collective-permute-start(bf16[2,1,384,768]{3,2,0,1:T(8,128)(2,1)S(1)} %get-tuple-element.115), channel_id=1, source_target_pairs={{12,0},{0,4},{4,8},{8,12},{13,1},{1,5},{5,9},{9,13},{14,2},{2,6},{... | collective-permute-start | bytes 3538952 | tf_op jit(solution)/shard_map/ppermute | solution.py:13
  30.0 52.6 %collective-permute-start.1 = (bf16[2,1,384,768]{3,2,0,1:T(8,128)(2,1)S(1)}, bf16[2,1,384,768]{3,2,0,1:T(8,128)(2,1)S(1)}, u32[]{:S(2)}, u32[]{:S(2)}) collective-permute-start(bf16[2,1,384,768]{3,2,0,1:T(8,128)(2,1)S(1)} %get-tuple-element.115), channel_id=1, source_target_pairs={{4,0},{8,4},{12,8},{0,12},{5,1},{9,5},{13,9},{1,13},{6,2},{10,6},{... | collective-permute-start | bytes 3538952 | tf_op jit(solution)/shard_map/ppermute | solution.py:13
  82.7 3.3 %copy-start = (bf16[96,3072]{1,0:T(8,128)(2,1)S(1)}, bf16[96,3072]{1,0:T(8,128)(2,1)}, u32[]{:S(2)}) copy-start(bf16[96,3072]{1,0:T(8,128)(2,1)} %param.8) | copy-start | bytes 1769476
  82.7 8.4 %copy-start.1 = (s32[1,27]{1,0:T(1,128)S(1)}, s32[1,27]{1,0:T(1,128)}, u32[]{:S(2)}) copy-start(s32[1,27]{1,0:T(1,128)} %param.11) | copy-start | bytes 328
  84.7 154.9 %collective-permute-start.2 = (bf16[3,2,1,384,768]{4,3,1,0,2:T(8,128)(2,1)}, bf16[3,2,1,384,768]{4,3,1,0,2:T(8,128)(2,1)}, u32[]{:S(2)}, u32[]{:S(2)}) collective-permute-start(bf16[3,2,1,384,768]{4,3,1,0,2:T(8,128)(2,1)} %get-tuple-element.113), channel_id=1, source_target_pairs={{8,0},{12,4},{0,8},{4,12},{9,1},{13,5},{1,9},{5,13},{10,2},{14,6},... | collective-permute-start | bytes 10616840 | tf_op jit(solution)/shard_map/ppermute | solution.py:13
  86.9 170.0 %all-to-all-start = ((bf16[96,4,768]{2,0,1:T(8,128)(2,1)}), bf16[96,4,768]{2,0,1:T(8,128)(2,1)}, u32[]{:S(2)}, u32[]{:S(2)}) async-start(bf16[96,4,768]{2,0,1:T(8,128)(2,1)} %bitcast.83), calls=%async_computation | async-start | bytes 1179648 | tf_op jit(solution)/shard_map/all_to_all | solution.py:21
where the time goes:
time: 328 us; the launch traced here: 327 us
  waiting for transfers between devices  207 us (63%)
  local copies, waits for them, and re-layouts  38.3 us (12%)
  blocking collectives  23.8 us (7%)
  matrix products  21.1 us (6%)
  other arithmetic  18.6 us (6%)
  starting transfers between devices  14.1 us (4%)
  loops' own time  4.07 us (1%)
    ppermute x3, waiting for transfers between devices, passed_along(): return lax.ppermute(block, axis, route)  199 us
    all_to_all x1, blocking collectives, on_device(): lax.all_to_all(result, 'head', split_axis=0, concat_axis=1, tiled=True)  11.9 us
    all_to_all x1, blocking collectives, on_device(): lax.all_to_all(value_rows, 'head', split_axis=1, concat_axis=0, tiled=True)  11.9 us
    dot_general x6, matrix products, one_head(): jnp.einsum('fqd,fkd->fqk', query_head, picked_keys, preferred_element_typ...  11.2 us
    another operation x2, other arithmetic, on_device(): window = jnp.stack([column_parts[0], row_strip, column_parts[1]])  10.4 us
    dot_general x6, matrix products, one_head(): jnp.einsum('fqk,fkd->fqd', rounded, picked_values, preferred_element_type...  9.83 us
    dynamic_slice x6, local copies, waits for them, and re-layouts, one_head(): value_head = lax.dynamic_slice_in_dim(value_tiles, column_start, HDIM, 2)  9.42 us
    slice x1, local copies, waits for them, and re-layouts, on_device(): value_tiles = window[:, :, 1].reshape(9 * frames, tile_len, feature_width)  8.9 us
  transfers between devices with their start and end apart: 5, of which 4 were waited for; matrix products, arithmetic and copies ran while one was open for 6% of the time, Pallas kernels for 0%

commit v1 on v0

--- a/solution.py
+++ b/solution.py
@@ -5,6 +5,30 @@
 from jax.sharding import PartitionSpec as P
 
 HDIM = 128
+
+
+def space_connect(target, axis_key):
+    view_out = lax.psum(1, axis_key)
+    current_block, local_now = (view_out, lax.axis_index(axis_key))
+    m_next = target.shape[1] // current_block
+    long_array = jnp.roll(target, shift=-local_now * m_next, axis=1)
+    tmp = lax.slice_in_dim(long_array, 0, m_next, axis=1)
+    grid = [tmp]
+    dev_j = 1
+    while dev_j < current_block:
+        all_values = lax.slice_in_dim(long_array, dev_j * m_next, (dev_j + 1) * m_next, axis=1)
+        grid.append(
+            lax.ppermute(
+                all_values,
+                axis_key,
+                [(t, (t + dev_j) % current_block) for t in range(current_block)],
+            )
+        )
+        dev_j = dev_j + 1
+    everything = jnp.roll(
+        jnp.concatenate(grid[::-1], axis=0), (local_now + 1) * grid[0].shape[0], axis=0
+    )
+    return everything
 
 
 def passed_along(block, axis, distance):
@@ -20,7 +44,7 @@
     query_local, key_local, value_local = (
         lax.all_to_all(query_rows, "head", split_axis=1, concat_axis=0, tiled=True),
         lax.all_to_all(key_rows, "head", split_axis=1, concat_axis=0, tiled=True),
-        lax.all_to_all(value_rows, "head", split_axis=1, concat_axis=0, tiled=True),
+        space_connect(value_rows, "head"),
     )
     feature_width = query_local.shape[1]
     head_count = feature_width // HDIM

time: 328 us -> 320 us (0.976)
  blocking collectives: 23.8 us -> 11.9 us
    all_to_all x1 -> x0, blocking collectives: 11.9 us -> none  [on_device(): lax.all_to_all(value_rows, 'head', split_axis=1, concat_axis=0, tiled=True)]
  transfers between devices with their start and end apart: 5 -> 8, of which waited for: 4 -> 5; matrix products, arithmetic and copies ran while one was open for 6% -> 6% of each run, Pallas kernels for 0% -> 0%
where the time goes in v1:
time: 320 us; the launch traced here: 319 us
  waiting for transfers between devices  208 us (65%)
  local copies, waits for them, and re-layouts  37.6 us (12%)
  matrix products  21 us (7%)
  other arithmetic  20.2 us (6%)
  starting transfers between devices  16.1 us (5%)
  blocking collectives  11.9 us (4%)
  loops' own time  4.4 us (1%)
    ppermute x3, waiting for transfers between devices, passed_along(): return lax.ppermute(block, axis, route)  199 us
    all_to_all x1, blocking collectives, on_device(): lax.all_to_all(result, 'head', split_axis=0, concat_axis=1, tiled=True)  11.9 us
    dot_general x6, matrix products, one_head(): jnp.einsum('fqd,fkd->fqk', query_head, picked_keys, preferred_element_typ...  11.2 us
    another operation x2, other arithmetic, on_device(): window = jnp.stack([column_parts[0], row_strip, column_parts[1]])  10.4 us
    dot_general x6, matrix products, one_head(): jnp.einsum('fqk,fkd->fqd', rounded, picked_values, preferred_element_type...  9.83 us
    dynamic_slice x6, local copies, waits for them, and re-layouts, one_head(): value_head = lax.dynamic_slice_in_dim(value_tiles, column_start, HDIM, 2)  9.44 us
    slice x1, local copies, waits for them, and re-layouts, on_device(): value_tiles = window[:, :, 1].reshape(9 * frames, tile_len, feature_width)  8.9 us
    all_to_all x1, waiting for transfers between devices, on_device(): lax.all_to_all(key_rows, 'head', split_axis=1, concat_axis=0, tiled=True)  7.13 us
  transfers between devices with their start and end apart: 8, of which 5 were waited for; matrix products, arithmetic and copies ran while one was open for 6% of the time, Pallas kernels for 0%

profile of v1, /device:TPU:0, one launch (start us, length us, event | category | flops | bytes accessed | tf_op | source)
XLA Modules:
  0.0 319.2 jit_solution(2125154517383322702)
XLA Ops:
  0.0 1.5 fusion.36
  1.6 2.5 collective-permute-start
  4.8 1.9 copy.37
  6.7 3.5 %all-to-all-start.1 = ((bf16[96,4,768]{2,0,1:T(8,128)(2,1)}), bf16[96,4,768]{2,0,1:T(8,128)(2,1)S(1)}, u32[]{:S(2)}, u32[]{:S(2)}) async-start(bf16[96,4,768]{2,0,1:T(8,128)(2,1)} %bitcast.52), calls=%async_computation.1 | async-start | bytes 1179648 | tf_op jit(solution)/shard_map/all_to_all | solution.py:46
  10.3 2.0 collective-permute-done.1
  12.6 7.1 %all-to-all-done.1 = bf16[96,4,768]{2,0,1:T(8,128)(2,1)S(1)} async-done(((bf16[96,4,768]{2,0,1:T(8,128)(2,1)}), bf16[96,4,768]{2,0,1:T(8,128)(2,1)S(1)}, u32[]{:S(2)}, u32[]{:S(2)}) %all-to-all-start.1) | async-done | bytes 589856 | tf_op jit(solution)/shard_map/all_to_all | solution.py:46
  19.9 1.6 collective-permute-start.3
  21.5 2.2 collective-permute-start.4
  23.7 26.9 %collective-permute-done.3 = bf16[2,1,384,768]{3,2,0,1:T(8,128)(2,1)S(1)} collective-permute-done((bf16[2,1,384,768]{3,2,0,1:T(8,128)(2,1)S(1)}, bf16[2,1,384,768]{3,2,0,1:T(8,128)(2,1)S(1)}, u32[]{:S(2)}, u32[]{:S(2)}) %collective-permute-start.3) | collective-permute-done | bytes 1179680 | tf_op jit(solution)/shard_map/ppermute | solution.py:37
  50.6 23.3 %collective-permute-done.4 = bf16[2,1,384,768]{3,2,0,1:T(8,128)(2,1)S(1)} collective-permute-done((bf16[2,1,384,768]{3,2,0,1:T(8,128)(2,1)S(1)}, bf16[2,1,384,768]{3,2,0,1:T(8,128)(2,1)S(1)}, u32[]{:S(2)}, u32[]{:S(2)}) %collective-permute-start.4) | collective-permute-done | bytes 1179680 | tf_op jit(solution)/shard_map/ppermute | solution.py:37
  73.9 2.0 fusion.32
  75.9 1.3 collective-permute-start.5
  77.2 0.9 copy.38
  78.1 4.2 %all-to-all-start = ((bf16[96,4,768]{2,0,1:T(8,128)(2,1)}), bf16[96,4,768]{2,0,1:T(8,128)(2,1)}, u32[]{:S(2)}, u32[]{:S(2)}) async-start(bf16[96,4,768]{2,0,1:T(8,128)(2,1)} %bitcast.77), calls=%async_computation | async-start | bytes 1179648 | tf_op jit(solution)/shard_map/all_to_all | solution.py:45
  82.4 148.5 %collective-permute-done.5 = bf16[3,2,1,384,768]{4,3,1,0,2:T(8,128)(2,1)} collective-permute-done((bf16[3,2,1,384,768]{4,3,1,0,2:T(8,128)(2,1)}, bf16[3,2,1,384,768]{4,3,1,0,2:T(8,128)(2,1)}, u32[]{:S(2)}, u32[]{:S(2)}) %collective-permute-start.5) | collective-permute-done | bytes 3538976 | tf_op jit(solution)/shard_map/ppermute | solution.py:37
  230.8 8.4 %pad_maximum_fusion = bf16[3,3,2,1,384,768]{5,4,2,1,3,0:T(8,128)(2,1)} fusion(bf16[1,3,2,1,384,768]{5,4,2,1,3,0:T(8,128)(2,1)} %bitcast.10, bf16[1,3,2,1,384,768]{5,4,2,1,3,0:T(8,128)(2,1)S(1)} %get-tuple-element.112), kind=kLoop, calls=%fused_computation.36 | loop fusion | flops 10616832 | bytes 17694720 | tf_op jit(solution)/shard_map/stack | solution.py:59
  239.3 8.9 %fusion.37 = (bf16[3,3,1,1,384,768]{5,4,2,1,3,0:T(8,128)(2,1)}, bf16[3,3,1,1,384,768]{5,4,2,1,3,0:T(8,128)(2,1)}) fusion(bf16[3,3,2,1,384,768]{5,4,2,1,3,0:T(8,128)(2,1)} %pad_maximum_fusion), kind=kLoop, calls=%fused_computation.59 | loop fusion | bytes 21233664 | tf_op jit(solution)/shard_map/slice | solution.py:61
  248.2 56.1 %while.12 = (s32[]{:T(128)}, bf16[6,1,384,128]{3,2,1,0:T(8,128)(2,1)}, s32[6]{0:T(128)S(1)}, bf16[384,768]{1,0:T(8,128)(2,1)}, bf16[9,384,768]{2,1,0:T(8,128)(2,...) while((s32[]{:T(128)}, ...), condition=%wide.region_3.5_spmd.clone.clone, body=%wide.region_0.4_spmd.clone.clone.sunk | while | flops 692404736 | bytes 28541528 | solution.py:99
  249.5 1.6 constant_dynamic-slice_fusion.3
  251.1 0.7 gather_fusion
  251.9 0.7 gather_fusion.1
  252.9 1.9 select_reduce_fusion.2
  254.8 1.1 fusion.51
  255.9 1.6 fusion.52
  258.9 1.6 constant_dynamic-slice_fusion.3
  262.3 1.9 select_reduce_fusion.2
  264.1 1.1 fusion.51
  265.2 1.6 fusion.52
  268.2 1.6 constant_dynamic-slice_fusion.3
  271.6 1.9 select_reduce_fusion.2
  273.5 1.1 fusion.51
  274.6 1.6 fusion.52
  277.6 1.6 constant_dynamic-slice_fusion.3
  281.0 1.9 select_reduce_fusion.2
  282.8 1.1 fusion.51
  283.9 1.6 fusion.52
  286.9 1.6 constant_dynamic-slice_fusion.3
  288.5 0.7 gather_fusion
  290.3 1.9 select_reduce_fusion.2
  292.2 1.1 fusion.51
  293.3 1.6 fusion.52
  296.2 1.6 constant_dynamic-slice_fusion.3
  299.6 1.9 select_reduce_fusion.2
  301.5 1.1 fusion.51
  302.6 1.6 fusion.52
  304.2 1.5 copy.30
  306.4 11.9 %all_to_all.54 = bf16[4,96,768]{2,1,0:T(8,128)(2,1)S(1)} all-to-all(bf16[4,96,768]{2,1,0:T(8,128)(2,1)S(1)} %all_to_all.47), channel_id=1, replica_groups=mesh['groups'=2,'ctx'=4,'head'=4] {'head'}, dimensions={0} | all-to-all | bytes 1179648 | tf_op jit(solution)/shard_map/all_to_all | solution.py:101
  318.3 0.9 copy.34
  (76 shorter events, 14.4 us)
Async XLA Ops:
  1.6 8.7 %collective-permute-start = (bf16[96,768]{1,0:T(8,128)(2,1)S(1)}, bf16[96,768]{1,0:T(8,128)(2,1)S(1)}, u32[]{:S(2)}, u32[]{:S(2)}) collective-permute-start(bf16[96,768]{1,0:T(8,128)(2,1)S(1)} %get-tuple-element.118), channel_id=1, source_target_pairs={{0,3},{1,0},{2,1},{3,2},{4,7},{5,4},{6,5},{7,6},{8,11},{9,8},{10,9... | collective-permute-start | bytes 442376 | tf_op jit(solution)/shard_map/ppermute | solution.py:21
  4.1 8.2 %collective-permute-start.1 = (bf16[96,768]{1,0:T(8,128)(2,1)S(1)}, bf16[96,768]{1,0:T(8,128)(2,1)S(1)}, u32[]{:S(2)}, u32[]{:S(2)}) collective-permute-start(bf16[96,768]{1,0:T(8,128)(2,1)S(1)} %get-tuple-element.117), channel_id=1, source_target_pairs={{0,2},{1,3},{2,0},{3,1},{4,6},{5,7},{6,4},{7,5},{8,10},{9,11},{10,... | collective-permute-start | bytes 442376 | tf_op jit(solution)/shard_map/ppermute | solution.py:21
  4.7 7.6 %collective-permute-start.2 = (bf16[96,768]{1,0:T(8,128)(2,1)S(1)}, bf16[96,768]{1,0:T(8,128)(2,1)S(1)}, u32[]{:S(2)}, u32[]{:S(2)}) collective-permute-start(bf16[96,768]{1,0:T(8,128)(2,1)S(1)} %get-tuple-element.116), channel_id=1, source_target_pairs={{0,1},{1,2},{2,3},{3,0},{4,5},{5,6},{6,7},{7,4},{8,9},{9,10},{10,1... | collective-permute-start | bytes 442376 | tf_op jit(solution)/shard_map/ppermute | solution.py:21
  6.7 13.0 %all-to-all-start.1 = ((bf16[96,4,768]{2,0,1:T(8,128)(2,1)}), bf16[96,4,768]{2,0,1:T(8,128)(2,1)S(1)}, u32[]{:S(2)}, u32[]{:S(2)}) async-start(bf16[96,4,768]{2,0,1:T(8,128)(2,1)} %bitcast.52), calls=%async_computation.1 | async-start | bytes 1179648 | tf_op jit(solution)/shard_map/all_to_all | solution.py:46
  19.9 30.7 %collective-permute-start.3 = (bf16[2,1,384,768]{3,2,0,1:T(8,128)(2,1)S(1)}, bf16[2,1,384,768]{3,2,0,1:T(8,128)(2,1)S(1)}, u32[]{:S(2)}, u32[]{:S(2)}) collective-permute-start(bf16[2,1,384,768]{3,2,0,1:T(8,128)(2,1)S(1)} %get-tuple-element.115), channel_id=1, source_target_pairs={{12,0},{0,4},{4,8},{8,12},{13,1},{1,5},{5,9},{9,13},{14,2},{2,6},{... | collective-permute-start | bytes 3538952 | tf_op jit(solution)/shard_map/ppermute | solution.py:37
  21.5 52.4 %collective-permute-start.4 = (bf16[2,1,384,768]{3,2,0,1:T(8,128)(2,1)S(1)}, bf16[2,1,384,768]{3,2,0,1:T(8,128)(2,1)S(1)}, u32[]{:S(2)}, u32[]{:S(2)}) collective-permute-start(bf16[2,1,384,768]{3,2,0,1:T(8,128)(2,1)S(1)} %get-tuple-element.115), channel_id=1, source_target_pairs={{4,0},{8,4},{12,8},{0,12},{5,1},{9,5},{13,9},{1,13},{6,2},{10,6},{... | collective-permute-start | bytes 3538952 | tf_op jit(solution)/shard_map/ppermute | solution.py:37
  73.9 3.3 %copy-start = (bf16[96,3072]{1,0:T(8,128)(2,1)S(1)}, bf16[96,3072]{1,0:T(8,128)(2,1)}, u32[]{:S(2)}) copy-start(bf16[96,3072]{1,0:T(8,128)(2,1)} %param.8) | copy-start | bytes 1769476
  73.9 8.4 %copy-start.1 = (s32[1,27]{1,0:T(1,128)S(1)}, s32[1,27]{1,0:T(1,128)}, u32[]{:S(2)}) copy-start(s32[1,27]{1,0:T(1,128)} %param.11) | copy-start | bytes 328
  75.9 154.9 %collective-permute-start.5 = (bf16[3,2,1,384,768]{4,3,1,0,2:T(8,128)(2,1)}, bf16[3,2,1,384,768]{4,3,1,0,2:T(8,128)(2,1)}, u32[]{:S(2)}, u32[]{:S(2)}) collective-permute-start(bf16[3,2,1,384,768]{4,3,1,0,2:T(8,128)(2,1)} %get-tuple-element.113), channel_id=1, source_target_pairs={{8,0},{12,4},{0,8},{4,12},{9,1},{13,5},{1,9},{5,13},{10,2},{14,6},... | collective-permute-start | bytes 10616840 | tf_op jit(solution)/shard_map/ppermute | solution.py:37
  78.1 170.1 %all-to-all-start = ((bf16[96,4,768]{2,0,1:T(8,128)(2,1)}), bf16[96,4,768]{2,0,1:T(8,128)(2,1)}, u32[]{:S(2)}, u32[]{:S(2)}) async-start(bf16[96,4,768]{2,0,1:T(8,128)(2,1)} %bitcast.77), calls=%async_computation | async-start | bytes 1179648 | tf_op jit(solution)/shard_map/all_to_all | solution.py:45
